TPU v7x, 768 devices: a whole 4x8x12 slice. The times are simulated.
768 devices in a mesh: tensor: 48 (over y_hi, z), context: 16 (over x, y_lo, core).
Axes of the slice: x: 4, y: 8 (y_hi: 4, y_lo: 2; y = y_hi * 2 + y_lo), z: 12, core: 2. Of those that a mesh axis runs over, the one named last changes fastest.
Arguments:
- tokens: bfloat16 [6144, 8192], P('context'), may hold values from -48 to 48
- w_query: bfloat16 [8192, 6144], P(None, 'tensor'), may hold values from -0.0625 to 0.0625
- w_key: bfloat16 [8192, 6144], P(None, 'tensor'), may hold values from -0.0625 to 0.0625
- w_value: bfloat16 [8192, 6144], P(None, 'tensor'), may hold values from -0.0625 to 0.0625
- mix_gate: bfloat16 [48, 96], replicated, may hold values from -0.875 to 0.875
- mix_up: bfloat16 [48, 96], replicated, may hold values from -0.875 to 0.875
- mix_down: bfloat16 [96, 48], replicated, may hold values from -0.625 to 0.625
- block_ids: int32 [64], P('context'), may hold values from 0 to 31, as said below
Outputs:
- attended: bfloat16 [6144, 6144], P('context', 'tensor')
Inputs may be any that keep to these rules, and one draw needn't show every extreme that they name: `block_ids`: device c of the context axis holds entries 4c to 4c+3: (a, 31 - a) for the first sequence and (b, 31 - b) for the second; over all devices each sequence's block numbers appear once each.
All inputs are finite; a program needn't handle non-finite values.
Results may differ from a plain program's by a relative error of at most 0.012.
The roundings to bfloat16 on the way count: a program that leaves them out, or rounds other values in their place, can miss the bound.
Values may be sent and summed in bfloat16 or wider, within the bound.
No kernel may reach another device: no remote copies, remote signals or barrier semaphores. Data moves between devices by JAX's collectives and lax.ppermute only.
A program may use at most 64 MiB of HBM per device.

v0:
```python
import jax
import jax.numpy as jnp
from jax import lax
from jax.experimental import pallas as pl
from jax.experimental.pallas import tpu as pltpu
from jax.sharding import PartitionSpec as P


HEAD_DIM = 128
BLK = 96
PAD = 16
CHUNKS = 8
STEPS = (0, 1, 3, 2)
CORE_GROUPS = [[2 * k + core for k in range(8)] for core in range(2)]
VMEM = pltpu.MemorySpace.VMEM
SMEM = pltpu.MemorySpace.SMEM
HBM = pltpu.MemorySpace.HBM
GRANT = pltpu.CompilerParams(vmem_limit_bytes=16 * 2**20)


def on_chip(x):
    return pltpu.with_memory_space_constraint(x, VMEM)


def off_chip(x):
    return pltpu.with_memory_space_constraint(x, HBM)


def in_vmem(shape, dtype):
    return pltpu.VMEM(shape, dtype)


def product(x_ref, kept, rest, refs, held, sems, fetch_kept):
    rows, width = x_ref.shape
    depth = width // CHUNKS
    half = CHUNKS // 2
    third = rows // 3

    def copies(k):
        at = pl.ds(k * depth, depth)
        found = [
            pltpu.make_async_copy(ref.at[at, :], keep.at[at, :], sems.at[n, k])
            for n, (ref, keep) in enumerate(zip(refs, held))
        ]
        if fetch_kept or k >= half:
            part = kept if k < half else rest
            to = pl.ds(k % half * depth, depth)
            found.append(pltpu.make_async_copy(x_ref.at[:, at], part.at[:, to], sems.at[2, k]))
        return found

    for k in range(CHUNKS):
        for copy in copies(k):
            copy.start()
    totals = [None] * 3
    for k in range(CHUNKS):
        for copy in copies(k):
            copy.wait()
        at = slice(k * depth, (k + 1) * depth)
        to = slice(k % half * depth, (k % half + 1) * depth)
        part = kept if k < half else rest
        sides = [keep[at, :] for keep in held]
        side = sides[0] if len(sides) == 1 else jnp.concatenate(sides, axis=1)
        for n in range(3):
            here = jnp.dot(
                part[n * third : (n + 1) * third, to], side, preferred_element_type=jnp.float32
            )
            totals[n] = here if totals[n] is None else totals[n] + here
    return jnp.concatenate(totals, axis=0)


def value_kernel(x_ref, w_ref, out_ref, kept_ref, rest, w_held, sems):
    total = product(x_ref, kept_ref, rest, [w_ref], [w_held], sems, True)
    out_ref[...] = total.astype(out_ref.dtype)


def project_values(tokens, w_value):
    rows, width = tokens.shape
    cols = w_value.shape[1]
    return pl.pallas_call(
        value_kernel,
        in_specs=[pl.BlockSpec(memory_space=HBM)] * 2,
        out_specs=[pl.BlockSpec(memory_space=VMEM)] * 2,
        out_shape=[
            in_vmem((rows, cols), jnp.bfloat16),
            in_vmem((rows, width // 2), jnp.bfloat16),
        ],
        scratch_shapes=[
            pltpu.VMEM((rows, width // 2), jnp.bfloat16),
            pltpu.VMEM(w_value.shape, jnp.bfloat16),
            pltpu.SemaphoreType.DMA((3, CHUNKS)),
        ],
        compiler_params=GRANT,
        name="project_values",
    )(off_chip(tokens), off_chip(w_value))


def query_key_kernel(
    ids_ref, x_ref, kept_ref, wq_ref, wk_ref, q_ref, k_ref, rest, q_held, k_held, sems
):
    rows, cols = q_ref.shape
    total = product(x_ref, kept_ref, rest, [wq_ref, wk_ref], [q_held, k_held], sems, False)
    q_ref[...] = total[:, :cols].astype(q_ref.dtype)
    k_ref[0, :rows, :] = total[:, cols:].astype(k_ref.dtype)
    row = lax.broadcasted_iota(jnp.int32, (PAD, cols), 0)
    ids = jnp.zeros((PAD, cols), jnp.float32)
    for j in range(4):
        ids = jnp.where(row == j, ids_ref[j].astype(jnp.float32), ids)
    k_ref[0, rows:, :] = ids.astype(k_ref.dtype)


def project_queries_keys(block_ids, tokens, kept, w_query, w_key):
    rows, width = tokens.shape
    cols = w_query.shape[1]
    return pl.pallas_call(
        query_key_kernel,
        in_specs=[
            pl.BlockSpec(memory_space=space) for space in (SMEM, HBM, VMEM, HBM, HBM)
        ],
        out_specs=[pl.BlockSpec(memory_space=VMEM)] * 2,
        out_shape=[
            pltpu.HBM((rows, cols), jnp.bfloat16),
            in_vmem((1, rows + PAD, cols), jnp.bfloat16),
        ],
        scratch_shapes=[
            pltpu.VMEM((rows, width // 2), jnp.bfloat16),
            pltpu.VMEM(w_query.shape, jnp.bfloat16),
            pltpu.VMEM(w_key.shape, jnp.bfloat16),
            pltpu.SemaphoreType.DMA((3, CHUNKS)),
        ],
        compiler_params=GRANT,
        name="project_queries_keys",
    )(off_chip(block_ids), off_chip(tokens), on_chip(kept), off_chip(w_query), off_chip(w_key))


def mix_kernel(u_ref, w_in_ref, w_out_ref, out_ref, wide_ref):
    count = u_ref.shape[1]
    hidden_units = w_in_ref.shape[0] // 2
    wide_ref[...] = u_ref[...].astype(jnp.float32)
    for first in range(0, count, 2):
        flat = jnp.concatenate([wide_ref[:, first + t, :] for t in range(2)], axis=1)
        parts = jnp.dot(
            w_in_ref[...], flat.astype(jnp.bfloat16), preferred_element_type=jnp.float32
        )
        hidden = (jax.nn.silu(parts[:hidden_units]) * parts[hidden_units:]).astype(jnp.bfloat16)
        mixed = flat + jnp.dot(w_out_ref[...], hidden, preferred_element_type=jnp.float32)
        for t in range(2):
            wide_ref[:, first + t, :] = mixed[:, t * HEAD_DIM : (t + 1) * HEAD_DIM]
    out_ref[...] = wide_ref[...].astype(out_ref.dtype)


def mix(gathered, w_in, w_out):
    return pl.pallas_call(
        mix_kernel,
        in_specs=[pl.BlockSpec(memory_space=VMEM)] * 3,
        out_specs=pl.BlockSpec(memory_space=VMEM),
        out_shape=in_vmem(gathered.shape, jnp.bfloat16),
        scratch_shapes=[pltpu.VMEM(gathered.shape, jnp.float32)],
        compiler_params=GRANT,
        name="mix_heads",
    )(on_chip(gathered), w_in, w_out)


def weight_kernel(ids_ref, q_ref, *refs):
    *key_refs, w_ref, total_ref, s_ref = refs
    half = q_ref.shape[0] // 2
    rows = q_ref.shape[0]
    chunk = 2 * half
    scale = HEAD_DIM ** (-0.5)
    q_row = lax.broadcasted_iota(jnp.int32, (half, 1), 0)
    lane = lax.broadcasted_iota(jnp.int32, (1, chunk), 1)
    lane_off = lane % BLK
    lane_blk = lane // BLK
    sources = [(k_ref, d) for k_ref in key_refs for d in range(k_ref.shape[0])]
    for s in range(2):
        id_lo, id_hi = ids_ref[2 * s], ids_ref[2 * s + 1]
        q_pos = jnp.where(q_row < BLK, id_lo * BLK + q_row, id_hi * BLK + q_row - BLK)
        queries = q_ref[s * half : (s + 1) * half, :]
        top = jnp.full((half, chunk), -1e30, jnp.float32)
        at = 0
        for first in range(0, len(sources), 2):
            pair = sources[first : first + 2]
            keys = jnp.concatenate(
                [k_ref[d, s * half : (s + 1) * half, :] for k_ref, d in pair], axis=0
            )
            k_ids = jnp.zeros((1, chunk), jnp.float32)
            for e, (k_ref, d) in enumerate(pair):
                tail = k_ref[d, rows:, :].astype(jnp.float32)
                for j in range(2):
                    wide = jnp.concatenate([tail[2 * s + j : 2 * s + j + 1, :]] * 3, axis=1)
                    k_ids = jnp.where(lane_blk == 2 * e + j, wide, k_ids)
            k_pos = k_ids.astype(jnp.int32) * BLK + lane_off
            scores = (
                lax.dot_general(
                    queries, keys, (((1,), (1,)), ((), ())), preferred_element_type=jnp.float32
                )
                * scale
            )
            scores = jnp.where(k_pos <= q_pos, scores, -1e30)
            s_ref[:, at : at + chunk] = scores
            top = jnp.maximum(top, scores)
            at += chunk
        top = jnp.max(top, axis=1, keepdims=True)
        total = jnp.zeros((half, chunk), jnp.float32)
        for at in range(0, s_ref.shape[1], chunk):
            weights = jnp.exp(s_ref[:, at : at + chunk] - top)
            total = total + weights
            w_ref[s, :, at : at + chunk] = weights.astype(w_ref.dtype)
        total = jnp.sum(total, axis=1, keepdims=True)
        total_ref[s * half : (s + 1) * half, :] = jnp.broadcast_to(total, (half, HEAD_DIM))


def attention_weights(block_ids, queries, keys):
    rows = queries.shape[0]
    half = rows // 2
    count = sum(piece.shape[0] for piece in keys) * half
    return pl.pallas_call(
        weight_kernel,
        in_specs=[pl.BlockSpec(memory_space=SMEM)]
        + [pl.BlockSpec(memory_space=VMEM)] * (1 + len(keys)),
        out_specs=[pl.BlockSpec(memory_space=VMEM)] * 2,
        out_shape=[
            in_vmem((2, half, count), jnp.bfloat16),
            pltpu.HBM((rows, HEAD_DIM), jnp.float32),
        ],
        scratch_shapes=[pltpu.VMEM((half, count), jnp.float32)],
        compiler_params=GRANT,
        name="attention_weights",
    )(off_chip(block_ids), off_chip(queries), *[on_chip(k) for k in keys])


def summed(w_ref, v_ref, s, first):
    half = w_ref.shape[1]
    sources = 4
    mine = lax.axis_index("context") // 2
    acc = jnp.zeros((half, HEAD_DIM), jnp.float32)
    for d in range(0, v_ref.shape[0], sources):
        spots = [mine ^ (2 * STEPS[e // 2] + e % 2) for e in range(d, d + sources)]
        values = jnp.concatenate(
            [v_ref[spot, s * half : (s + 1) * half, :] for spot in spots], axis=0
        )
        at = first + d * half
        acc = acc + jnp.dot(
            w_ref[s, :, at : at + sources * half], values, preferred_element_type=jnp.float32
        )
    return acc


def first_kernel(w_ref, total_ref, v_ref, part_ref, kept_ref):
    half = w_ref.shape[1]
    for s in range(2):
        part_ref[s * half : (s + 1) * half, :] = summed(w_ref, v_ref, s, 0)
    kept_ref[...] = total_ref[...]


def last_kernel(w_ref, total_ref, part_ref, v_ref, out_ref):
    half = w_ref.shape[1]
    for s in range(2):
        rows = slice(s * half, (s + 1) * half)
        acc = part_ref[rows, :] + summed(w_ref, v_ref, s, w_ref.shape[2] // 2)
        out_ref[rows, :] = (acc / total_ref[rows, :]).astype(out_ref.dtype)


def apply_first(weights, total, values):
    return pl.pallas_call(
        first_kernel,
        in_specs=[pl.BlockSpec(memory_space=VMEM)] * 3,
        out_specs=[pl.BlockSpec(memory_space=VMEM)] * 2,
        out_shape=[in_vmem(total.shape, jnp.float32)] * 2,
        compiler_params=GRANT,
        name="apply_first",
    )(weights, off_chip(total), on_chip(values))


def apply_last(weights, total, part, values):
    return pl.pallas_call(
        last_kernel,
        in_specs=[pl.BlockSpec(memory_space=VMEM)] * 4,
        out_specs=pl.BlockSpec(memory_space=VMEM),
        out_shape=jax.ShapeDtypeStruct(total.shape, jnp.bfloat16),
        compiler_params=GRANT,
        name="apply_last",
    )(weights, total, part, on_chip(values))


def pack_kernel(*refs):
    *pieces, out_ref = refs
    n = 0
    for piece in pieces:
        out_ref[n : n + piece.shape[0]] = piece[...]
        n += piece.shape[0]


def pack(*pieces):
    count = sum(piece.shape[0] for piece in pieces)
    return pl.pallas_call(
        pack_kernel,
        in_specs=[pl.BlockSpec(memory_space=VMEM)] * len(pieces),
        out_specs=pl.BlockSpec(memory_space=VMEM),
        out_shape=in_vmem((count, *pieces[0].shape[1:]), pieces[0].dtype),
        compiler_params=GRANT,
        name="pack",
    )(*[on_chip(piece) for piece in pieces])


def repeat_kernel(x_ref, out_ref, sems):
    copies = [
        pltpu.make_async_copy(x_ref, out_ref.at[n], sems.at[n]) for n in range(out_ref.shape[0])
    ]
    for copy in copies:
        copy.start()
    for copy in copies:
        copy.wait()


def repeat(x, count):
    return pl.pallas_call(
        repeat_kernel,
        in_specs=[pl.BlockSpec(memory_space=VMEM)],
        out_specs=pl.BlockSpec(memory_space=HBM),
        out_shape=pltpu.HBM((count, *x.shape), x.dtype),
        scratch_shapes=[pltpu.SemaphoreType.DMA((count,))],
        compiler_params=GRANT,
        name="repeat",
    )(on_chip(x))


def shards(tokens, w_query, w_key, w_value, mix_gate, mix_up, mix_down, block_ids):
    heads = mix_gate.shape[0]
    rows = tokens.shape[0]

    def exchange(x):
        return lax.all_to_all(x, "tensor", split_axis=0, concat_axis=0, tiled=True)

    def spread(x):
        return lax.all_to_all(
            x, "context", split_axis=0, concat_axis=0, axis_index_groups=CORE_GROUPS, tiled=True
        )

    def flip(x, bit):
        return lax.ppermute(x, "context", [(i, i ^ bit) for i in range(16)])

    w_in = jnp.concatenate([mix_gate, mix_up], axis=1).T
    w_out = mix_down.T
    values, kept = project_values(tokens, w_value)
    gathered = exchange(values.reshape(heads, rows // heads, HEAD_DIM))
    queries, own = project_queries_keys(block_ids, tokens, kept, w_query, w_key)
    beside = flip(own, 2)
    mixed = mix(gathered, w_in, w_out)
    mixed_rows = exchange(mixed).reshape(rows, HEAD_DIM)
    pair = pack(own, beside)
    near = flip(pair, 4)
    wrap = flip(pair, 12)
    far = flip(pair, 8)
    keys = pack(pair, near, wrap, far)
    other_keys = flip(keys, 1)
    weights, total = attention_weights(block_ids, queries, [keys, other_keys])
    copies = repeat(mixed_rows, 8)
    values_mine = spread(copies)
    values_other = flip(values_mine, 1)
    part, total = apply_first(weights, total, values_mine)
    return apply_last(weights, total, part, values_other)


def solution(mesh):
    in_specs = (
        P("context", None),
        P(None, "tensor"),
        P(None, "tensor"),
        P(None, "tensor"),
        P(),
        P(),
        P(),
        P("context"),
    )
    out_specs = P("context", "tensor")
    return jax.shard_map(shards, mesh=mesh, in_specs=in_specs, out_specs=out_specs, check_vma=False)
```

profile of v0, /device:TPU:1, one launch (start us, length us, event | category | flops | bytes accessed | tf_op | source)
XLA Modules:
  0.0 111.9 jit_solution(11055117936437791783)
XLA Ops:
  0.0 0.0 copy-start.3
  0.0 0.0 copy-start.4
  0.0 0.0 copy-start.2
  0.0 5.2 %project_values.1 = (bf16[384,128]{1,0:T(8,128)(2,1)}, bf16[384,4096]{1,0:T(8,128)(2,1)S(1)}) custom-call(bf16[384,8192]{1,0:T(8,128)(2,1)} %x_ref.3, bf16[8192,128]{1,0:T(8,128)(2,1)} %w_ref.1), custom_call_target="tpu_custom_call" | custom-call | tf_op jit(solution)/shard_map/project_values/pallas_call | solution.py:79
  5.2 0.0 copy-start
  5.2 1.6 %copy-done = bf16[384,4096]{1,0:T(8,128)(2,1)} copy-done((bf16[384,4096]{1,0:T(8,128)(2,1)}, bf16[384,4096]{1,0:T(8,128)(2,1)S(1)}, u32[]{:S(2)}) %copy-start) | copy-done | bytes 3145752
  6.8 21.6 %all-to-all-start = ((bf16[48,8,128]{2,1,0:T(8,128)(2,1)}), bf16[48,8,128]{2,1,0:T(8,128)(2,1)S(1)}, u32[]{:S(2)}, u32[]{:S(2)}) async-start(bf16[48,8,128]{2,1,0:T(8,128)(2,1)} %bitcast), calls=%async_computation | async-start | bytes 196608 | tf_op jit(solution)/shard_map/all_to_all | solution.py:332
  28.5 0.0 copy-done.3
  28.5 0.1 copy.10
  28.6 0.0 copy-done.4
  28.6 0.1 copy.9
  28.7 14.0 %all-to-all-done.u_ref = bf16[48,8,128]{2,1,0:T(8,128)(2,1)S(1)} async-done(((bf16[48,8,128]{2,1,0:T(8,128)(2,1)}), bf16[48,8,128]{2,1,0:T(8,128)(2,1)S(1)}, u32[]{:S(2)}, u32[]{:S(2)}) %all-to-all-start) | async-done | bytes 98336 | tf_op jit(solution)/shard_map/all_to_all | solution.py:332
  42.7 0.0 copy-done.2
  42.7 0.9 mix_heads.1
  43.7 18.3 %all_to_all.15 = bf16[48,8,128]{2,1,0:T(8,128)(2,1)S(1)} all-to-all(bf16[48,8,128]{2,1,0:T(8,128)(2,1)S(1)} %mix_heads.1), channel_id=1, replica_groups=mesh['tensor'=48,'context'=16] {'tensor'}, dimensions={0} | all-to-all | bytes 196608 | tf_op jit(solution)/shard_map/all_to_all | solution.py:332
  61.9 1.0 repeat.1
  62.9 3.9 %all-to-all-start.2 = ((bf16[8,384,128]{2,1,0:T(8,128)(2,1)}), bf16[8,384,128]{2,1,0:T(8,128)(2,1)S(1)}, u32[]{:S(2)}, u32[]{:S(2)}) async-start(bf16[8,384,128]{2,1,0:T(8,128)(2,1)} %repeat.1), calls=%async_computation.2 | async-start | bytes 1572864 | tf_op jit(solution)/shard_map/all_to_all | solution.py:335
  66.8 0.0 copy-start.1
  66.8 1.9 %copy-done.1 = bf16[384,4096]{1,0:T(8,128)(2,1)S(1)} copy-done((bf16[384,4096]{1,0:T(8,128)(2,1)S(1)}, bf16[384,4096]{1,0:T(8,128)(2,1)}, u32[]{:S(2)}) %copy-start.1) | copy-done | bytes 3145752
  68.7 5.7 %project_queries_keys.1 = (bf16[384,128]{1,0:T(8,128)(2,1)}, bf16[1,400,128]{2,1,0:T(8,128)(2,1)S(1)}) custom-call(s32[4]{0:T(128)} %ids_ref.3, bf16[384,8192]{1,0:T(8,128)(2,1)} %x_ref.3, bf16[384,4096]{1,0:T(8,128)(2,1)S(1)} %copy-done.1, bf16[8192,128]{1,0:T(8,128)(2,1)} %wq_ref.1, bf16[8192,128]{1,0:T(8,128)(2,1)} %wk_ref.1), custom_call_target="tpu_custom_call" | custom-call | tf_op jit(solution)/shard_map/project_queries_keys/pallas_call | solution.py:114
  74.4 3.4 %collective-permute-start = (bf16[1,400,128]{2,1,0:T(8,128)(2,1)S(1)}, bf16[1,400,128]{2,1,0:T(8,128)(2,1)S(1)}, u32[]{:S(2)}, u32[]{:S(2)}) collective-permute-start(bf16[1,400,128]{2,1,0:T(8,128)(2,1)S(1)} %get-tuple-element.15.refs_0_), channel_id=1, source_target_pairs={{0,2},{1,3},{2,0},{3,1},{4,6},{5,7},{6,4},{7,5},{8,10},{9,11},{10,... | collective-permute-start | bytes 307208 | tf_op jit(solution)/shard_map/ppermute | solution.py:340
  77.8 2.3 %collective-permute-done.refs_1_ = bf16[1,400,128]{2,1,0:T(8,128)(2,1)S(1)} collective-permute-done((bf16[1,400,128]{2,1,0:T(8,128)(2,1)S(1)}, bf16[1,400,128]{2,1,0:T(8,128)(2,1)S(1)}, u32[]{:S(2)}, u32[]{:S(2)}) %collective-permute-start) | collective-permute-done | bytes 102432 | tf_op jit(solution)/shard_map/ppermute | solution.py:340
  80.1 3.1 %collective-permute-start.1 = (bf16[2,400,128]{2,1,0:T(8,128)(2,1)S(1)}, bf16[2,400,128]{2,1,0:T(8,128)(2,1)S(1)}, u32[]{:S(2)}, u32[]{:S(2)}) collective-permute-start(bf16[2,400,128]{2,1,0:T(8,128)(2,1)S(1)} %pack.2.refs_0_), channel_id=1, source_target_pairs={{0,4},{1,5},{2,6},{3,7},{4,0},{5,1},{6,2},{7,3},{8,12},{9,13},{10,... | collective-permute-start | bytes 614408 | tf_op jit(solution)/shard_map/ppermute | solution.py:340
  83.2 3.7 %collective-permute-start.2 = (bf16[2,400,128]{2,1,0:T(8,128)(2,1)S(1)}, bf16[2,400,128]{2,1,0:T(8,128)(2,1)S(1)}, u32[]{:S(2)}, u32[]{:S(2)}) collective-permute-start(bf16[2,400,128]{2,1,0:T(8,128)(2,1)S(1)} %pack.2.refs_0_), channel_id=1, source_target_pairs={{0,12},{1,13},{2,14},{3,15},{4,8},{5,9},{6,10},{7,11},{8,4},{9,5},... | collective-permute-start | bytes 614408 | tf_op jit(solution)/shard_map/ppermute | solution.py:340
  86.9 2.5 %collective-permute-start.3 = (bf16[2,400,128]{2,1,0:T(8,128)(2,1)S(1)}, bf16[2,400,128]{2,1,0:T(8,128)(2,1)S(1)}, u32[]{:S(2)}, u32[]{:S(2)}) collective-permute-start(bf16[2,400,128]{2,1,0:T(8,128)(2,1)S(1)} %pack.2.refs_0_), channel_id=1, source_target_pairs={{0,8},{1,9},{2,10},{3,11},{4,12},{5,13},{6,14},{7,15},{8,0},{9,1},... | collective-permute-start | bytes 614408 | tf_op jit(solution)/shard_map/ppermute | solution.py:340
  89.5 0.0 collective-permute-done.1.refs_1_
  89.5 1.5 %collective-permute-done.2.refs_2_ = bf16[2,400,128]{2,1,0:T(8,128)(2,1)S(1)} collective-permute-done((bf16[2,400,128]{2,1,0:T(8,128)(2,1)S(1)}, bf16[2,400,128]{2,1,0:T(8,128)(2,1)S(1)}, u32[]{:S(2)}, u32[]{:S(2)}) %collective-permute-start.2) | collective-permute-done | bytes 204832 | tf_op jit(solution)/shard_map/ppermute | solution.py:340
  90.9 5.8 %collective-permute-done.3.refs_3_ = bf16[2,400,128]{2,1,0:T(8,128)(2,1)S(1)} collective-permute-done((bf16[2,400,128]{2,1,0:T(8,128)(2,1)S(1)}, bf16[2,400,128]{2,1,0:T(8,128)(2,1)S(1)}, u32[]{:S(2)}, u32[]{:S(2)}) %collective-permute-start.3) | collective-permute-done | bytes 204832 | tf_op jit(solution)/shard_map/ppermute | solution.py:340
  96.8 0.1 pack.3.refs_0_
  96.8 7.1 %collective-permute-start.4 = (bf16[8,400,128]{2,1,0:T(8,128)(2,1)S(1)}, bf16[8,400,128]{2,1,0:T(8,128)(2,1)S(1)}, u32[]{:S(2)}, u32[]{:S(2)}) collective-permute-start(bf16[8,400,128]{2,1,0:T(8,128)(2,1)S(1)} %pack.3.refs_0_), channel_id=1, source_target_pairs={{0,1},{1,0},{2,3},{3,2},{4,5},{5,4},{6,7},{7,6},{8,9},{9,8},{10,11... | collective-permute-start | bytes 2457608 | tf_op jit(solution)/shard_map/ppermute | solution.py:340
  103.9 0.0 all-to-all-done.2.v_ref
  103.9 1.9 %collective-permute-start.5 = (bf16[8,384,128]{2,1,0:T(8,128)(2,1)S(1)}, bf16[8,384,128]{2,1,0:T(8,128)(2,1)S(1)}, u32[]{:S(2)}, u32[]{:S(2)}) collective-permute-start(bf16[8,384,128]{2,1,0:T(8,128)(2,1)S(1)} %all-to-all-done.2.v_ref), channel_id=1, source_target_pairs={{0,1},{1,0},{2,3},{3,2},{4,5},{5,4},{6,7},{7,6},{8,9},{9,8},{10,11... | collective-permute-start | bytes 2359304 | tf_op jit(solution)/shard_map/ppermute | solution.py:340
  105.8 0.0 collective-permute-done.4.refs_1_
  105.8 3.6 %attention_weights.1 = (bf16[2,192,3072]{2,1,0:T(8,128)(2,1)S(1)}, f32[384,128]{1,0:T(8,128)}) custom-call(s32[4]{0:T(128)} %ids_ref.3, bf16[384,128]{1,0:T(8,128)(2,1)} %get-tuple-element.14.q_ref, bf16[8,400,128]{2,1,0:T(8,128)(2,1)S(1)} %pack.3.refs_0_, bf16[8,400,128]{2,1,0:T(8,128)(2,1)S(1)} %collective-permute-done.4.refs_1_), custom_call_target="tpu_custom_call" | custom-call | tf_op jit(solution)/shard_map/attention_weights/pallas_call | solution.py:216
  109.4 1.4 %apply_first.1 = (f32[384,128]{1,0:T(8,128)S(1)}, f32[384,128]{1,0:T(8,128)S(1)}) custom-call(bf16[2,192,3072]{2,1,0:T(8,128)(2,1)S(1)} %get-tuple-element.16.w_ref, f32[384,128]{1,0:T(8,128)} %get-tuple-element.17.total_ref, bf16[8,384,128]{2,1,0:T(8,128)(2,1)S(1)} %all-to-all-done.2.v_ref), custom_call_target="tpu_custom_call" | custom-call | tf_op jit(solution)/shard_map/apply_first/pallas_call | solution.py:264
  110.8 0.0 collective-permute-done.5.v_ref
  110.8 1.1 %apply_last.1 = bf16[384,128]{1,0:T(8,128)(2,1)} custom-call(bf16[2,192,3072]{2,1,0:T(8,128)(2,1)S(1)} %get-tuple-element.16.w_ref, f32[384,128]{1,0:T(8,128)S(1)} %get-tuple-element.19.total_ref, f32[384,128]{1,0:T(8,128)S(1)} %get-tuple-element.20.part_ref, bf16[8,384,128]{2,1,0:T(8,128)(2,1)S(1)} %collective-permute-done.5.v_ref), custom_call_target="tpu_custom_call" | custom-call | tf_op jit(solution)/shard_map/apply_last/pallas_call | solution.py:275
  (2 shorter events, 0.0 us)
Async XLA Ops:
  0.0 28.5 %copy-start.3 = (bf16[48,96]{1,0:T(8,128)(2,1)S(1)}, bf16[48,96]{1,0:T(8,128)(2,1)}, u32[]{:S(2)}) copy-start(bf16[48,96]{1,0:T(8,128)(2,1)} %param.13) | copy-start | bytes 27652
  0.0 28.6 %copy-start.4 = (bf16[48,96]{1,0:T(8,128)(2,1)S(1)}, bf16[48,96]{1,0:T(8,128)(2,1)}, u32[]{:S(2)}) copy-start(bf16[48,96]{1,0:T(8,128)(2,1)} %param.12) | copy-start | bytes 27652
  0.0 42.7 %copy-start.2 = (bf16[96,48]{0,1:T(8,128)(2,1)S(1)}, bf16[96,48]{0,1:T(8,128)(2,1)}, u32[]{:S(2)}) copy-start(bf16[96,48]{0,1:T(8,128)(2,1)} %param.14) | copy-start | bytes 27652
  5.2 1.6 %copy-start = (bf16[384,4096]{1,0:T(8,128)(2,1)}, bf16[384,4096]{1,0:T(8,128)(2,1)S(1)}, u32[]{:S(2)}) copy-start(bf16[384,4096]{1,0:T(8,128)(2,1)S(1)} %get-tuple-element.13.kept_ref) | copy-start | bytes 9437188
  6.8 35.9 %all-to-all-start = ((bf16[48,8,128]{2,1,0:T(8,128)(2,1)}), bf16[48,8,128]{2,1,0:T(8,128)(2,1)S(1)}, u32[]{:S(2)}, u32[]{:S(2)}) async-start(bf16[48,8,128]{2,1,0:T(8,128)(2,1)} %bitcast), calls=%async_computation | async-start | bytes 196608 | tf_op jit(solution)/shard_map/all_to_all | solution.py:332
  62.9 41.0 %all-to-all-start.2 = ((bf16[8,384,128]{2,1,0:T(8,128)(2,1)}), bf16[8,384,128]{2,1,0:T(8,128)(2,1)S(1)}, u32[]{:S(2)}, u32[]{:S(2)}) async-start(bf16[8,384,128]{2,1,0:T(8,128)(2,1)} %repeat.1), calls=%async_computation.2 | async-start | bytes 1572864 | tf_op jit(solution)/shard_map/all_to_all | solution.py:335
  66.8 1.9 %copy-start.1 = (bf16[384,4096]{1,0:T(8,128)(2,1)S(1)}, bf16[384,4096]{1,0:T(8,128)(2,1)}, u32[]{:S(2)}) copy-start(bf16[384,4096]{1,0:T(8,128)(2,1)} %copy-done) | copy-start | bytes 9437188
  74.4 5.7 %collective-permute-start = (bf16[1,400,128]{2,1,0:T(8,128)(2,1)S(1)}, bf16[1,400,128]{2,1,0:T(8,128)(2,1)S(1)}, u32[]{:S(2)}, u32[]{:S(2)}) collective-permute-start(bf16[1,400,128]{2,1,0:T(8,128)(2,1)S(1)} %get-tuple-element.15.refs_0_), channel_id=1, source_target_pairs={{0,2},{1,3},{2,0},{3,1},{4,6},{5,7},{6,4},{7,5},{8,10},{9,11},{10,... | collective-permute-start | bytes 307208 | tf_op jit(solution)/shard_map/ppermute | solution.py:340
  80.1 9.3 %collective-permute-start.1 = (bf16[2,400,128]{2,1,0:T(8,128)(2,1)S(1)}, bf16[2,400,128]{2,1,0:T(8,128)(2,1)S(1)}, u32[]{:S(2)}, u32[]{:S(2)}) collective-permute-start(bf16[2,400,128]{2,1,0:T(8,128)(2,1)S(1)} %pack.2.refs_0_), channel_id=1, source_target_pairs={{0,4},{1,5},{2,6},{3,7},{4,0},{5,1},{6,2},{7,3},{8,12},{9,13},{10,... | collective-permute-start | bytes 614408 | tf_op jit(solution)/shard_map/ppermute | solution.py:340
  83.2 7.7 %collective-permute-start.2 = (bf16[2,400,128]{2,1,0:T(8,128)(2,1)S(1)}, bf16[2,400,128]{2,1,0:T(8,128)(2,1)S(1)}, u32[]{:S(2)}, u32[]{:S(2)}) collective-permute-start(bf16[2,400,128]{2,1,0:T(8,128)(2,1)S(1)} %pack.2.refs_0_), channel_id=1, source_target_pairs={{0,12},{1,13},{2,14},{3,15},{4,8},{5,9},{6,10},{7,11},{8,4},{9,5},... | collective-permute-start | bytes 614408 | tf_op jit(solution)/shard_map/ppermute | solution.py:340
  86.9 9.8 %collective-permute-start.3 = (bf16[2,400,128]{2,1,0:T(8,128)(2,1)S(1)}, bf16[2,400,128]{2,1,0:T(8,128)(2,1)S(1)}, u32[]{:S(2)}, u32[]{:S(2)}) collective-permute-start(bf16[2,400,128]{2,1,0:T(8,128)(2,1)S(1)} %pack.2.refs_0_), channel_id=1, source_target_pairs={{0,8},{1,9},{2,10},{3,11},{4,12},{5,13},{6,14},{7,15},{8,0},{9,1},... | collective-permute-start | bytes 614408 | tf_op jit(solution)/shard_map/ppermute | solution.py:340
  96.8 9.0 %collective-permute-start.4 = (bf16[8,400,128]{2,1,0:T(8,128)(2,1)S(1)}, bf16[8,400,128]{2,1,0:T(8,128)(2,1)S(1)}, u32[]{:S(2)}, u32[]{:S(2)}) collective-permute-start(bf16[8,400,128]{2,1,0:T(8,128)(2,1)S(1)} %pack.3.refs_0_), channel_id=1, source_target_pairs={{0,1},{1,0},{2,3},{3,2},{4,5},{5,4},{6,7},{7,6},{8,9},{9,8},{10,11... | collective-permute-start | bytes 2457608 | tf_op jit(solution)/shard_map/ppermute | solution.py:340
  103.9 6.9 %collective-permute-start.5 = (bf16[8,384,128]{2,1,0:T(8,128)(2,1)S(1)}, bf16[8,384,128]{2,1,0:T(8,128)(2,1)S(1)}, u32[]{:S(2)}, u32[]{:S(2)}) collective-permute-start(bf16[8,384,128]{2,1,0:T(8,128)(2,1)S(1)} %all-to-all-done.2.v_ref), channel_id=1, source_target_pairs={{0,1},{1,0},{2,3},{3,2},{4,5},{5,4},{6,7},{7,6},{8,9},{9,8},{10,11... | collective-permute-start | bytes 2359304 | tf_op jit(solution)/shard_map/ppermute | solution.py:340
where the time goes:
time: 112 us
  starting transfers between devices  47.2 us (42%)
  waiting for transfers between devices  23.6 us (21%)
  Pallas kernels  18.9 us (17%)
  blocking collectives  18.3 us (16%)
  local copies, waits for them, and re-layouts  3.75 us (3%)
    all_to_all x1, starting transfers between devices, exchange(): return lax.all_to_all(x, 'tensor', split_axis=0, concat_axis=0, tiled=True)  21.6 us
    ppermute x6, starting transfers between devices, flip(): return lax.ppermute(x, 'context', [(i, i ^ bit) for i in range(16)])  21.6 us
    all_to_all x1, blocking collectives, exchange(): return lax.all_to_all(x, 'tensor', split_axis=0, concat_axis=0, tiled=True)  18.3 us
    all_to_all x1, waiting for transfers between devices, exchange(): return lax.all_to_all(x, 'tensor', split_axis=0, concat_axis=0, tiled=True)  14 us
    ppermute x6, waiting for transfers between devices, flip(): return lax.ppermute(x, 'context', [(i, i ^ bit) for i in range(16)])  9.62 us
    pallas_call x1, Pallas kernels, project_queries_keys(): pl.pallas_call(query_key_kernel, in_specs=[pl.BlockSpec(memory_space=spac...  5.68 us
    pallas_call x1, Pallas kernels, project_values(): pl.pallas_call(value_kernel, in_specs=[pl.BlockSpec(memory_space=HBM)] *...  5.15 us
    all_to_all x1, starting transfers between devices, spread(): lax.all_to_all(x, 'context', split_axis=0, concat_axis=0, axis_index_grou...  3.94 us
  transfers between devices with their start and end apart: 8, of which 4 were waited for; matrix products, arithmetic and copies ran while one was open for 0% of the time, Pallas kernels for 10%

commit v1 on v0

--- a/solution.py
+++ b/solution.py
@@ -136,15 +136,12 @@
     count = u_ref.shape[1]
     hidden_units = w_in_ref.shape[0] // 2
     wide_ref[...] = u_ref[...].astype(jnp.float32)
-    for first in range(0, count, 2):
-        flat = jnp.concatenate([wide_ref[:, first + t, :] for t in range(2)], axis=1)
-        parts = jnp.dot(
-            w_in_ref[...], flat.astype(jnp.bfloat16), preferred_element_type=jnp.float32
-        )
-        hidden = (jax.nn.silu(parts[:hidden_units]) * parts[hidden_units:]).astype(jnp.bfloat16)
-        mixed = flat + jnp.dot(w_out_ref[...], hidden, preferred_element_type=jnp.float32)
-        for t in range(2):
-            wide_ref[:, first + t, :] = mixed[:, t * HEAD_DIM : (t + 1) * HEAD_DIM]
+    flat = jnp.concatenate([wide_ref[:, t, :] for t in range(count)], axis=1)
+    parts = jnp.dot(w_in_ref[...], flat.astype(jnp.bfloat16), preferred_element_type=jnp.float32)
+    hidden = (jax.nn.silu(parts[:hidden_units]) * parts[hidden_units:]).astype(jnp.bfloat16)
+    mixed = flat + jnp.dot(w_out_ref[...], hidden, preferred_element_type=jnp.float32)
+    for t in range(count):
+        wide_ref[:, t, :] = mixed[:, t * HEAD_DIM : (t + 1) * HEAD_DIM]
     out_ref[...] = wide_ref[...].astype(out_ref.dtype)
 
 
@@ -230,7 +227,7 @@
 
 def summed(w_ref, v_ref, s, first):
     half = w_ref.shape[1]
-    sources = 4
+    sources = 8
     mine = lax.axis_index("context") // 2
     acc = jnp.zeros((half, HEAD_DIM), jnp.float32)
     for d in range(0, v_ref.shape[0], sources):

time: 112 us -> 112 us (level)
  no operation moved by 1% of the time
where the time goes in v1:
time: 112 us
  starting transfers between devices  47.2 us (42%)
  waiting for transfers between devices  23.6 us (21%)
  Pallas kernels  18.4 us (16%)
  blocking collectives  18.3 us (16%)
  local copies, waits for them, and re-layouts  3.75 us (3%)
    ppermute x6, starting transfers between devices, flip(): return lax.ppermute(x, 'context', [(i, i ^ bit) for i in range(16)])  21.6 us
    all_to_all x1, starting transfers between devices, exchange(): return lax.all_to_all(x, 'tensor', split_axis=0, concat_axis=0, tiled=True)  21.6 us
    all_to_all x1, blocking collectives, exchange(): return lax.all_to_all(x, 'tensor', split_axis=0, concat_axis=0, tiled=True)  18.3 us
    all_to_all x1, waiting for transfers between devices, exchange(): return lax.all_to_all(x, 'tensor', split_axis=0, concat_axis=0, tiled=True)  14 us
    ppermute x6, waiting for transfers between devices, flip(): return lax.ppermute(x, 'context', [(i, i ^ bit) for i in range(16)])  9.62 us
    pallas_call x1, Pallas kernels, project_queries_keys(): pl.pallas_call(query_key_kernel, in_specs=[pl.BlockSpec(memory_space=spac...  5.69 us
    pallas_call x1, Pallas kernels, project_values(): pl.pallas_call(value_kernel, in_specs=[pl.BlockSpec(memory_space=HBM)] *...  5.15 us
    all_to_all x1, starting transfers between devices, spread(): lax.all_to_all(x, 'context', split_axis=0, concat_axis=0, axis_index_grou...  3.94 us
  transfers between devices with their start and end apart: 8, of which 4 were waited for; matrix products, arithmetic and copies ran while one was open for 0% of the time, Pallas kernels for 10%

profile of v1, /device:TPU:1, one launch (start us, length us, event | category | flops | bytes accessed | tf_op | source)
XLA Modules:
  0.0 111.5 jit_solution(3100938516903079981)
XLA Ops:
  0.0 0.0 copy-start.3
  0.0 0.0 copy-start.4
  0.0 0.0 copy-start.2
  0.0 5.2 %project_values.1 = (bf16[384,128]{1,0:T(8,128)(2,1)}, bf16[384,4096]{1,0:T(8,128)(2,1)S(1)}) custom-call(bf16[384,8192]{1,0:T(8,128)(2,1)} %x_ref.3, bf16[8192,128]{1,0:T(8,128)(2,1)} %w_ref.1), custom_call_target="tpu_custom_call" | custom-call | tf_op jit(solution)/shard_map/project_values/pallas_call | solution.py:79
  5.2 0.0 copy-start
  5.2 1.6 %copy-done = bf16[384,4096]{1,0:T(8,128)(2,1)} copy-done((bf16[384,4096]{1,0:T(8,128)(2,1)}, bf16[384,4096]{1,0:T(8,128)(2,1)S(1)}, u32[]{:S(2)}) %copy-start) | copy-done | bytes 3145752
  6.8 21.6 %all-to-all-start = ((bf16[48,8,128]{2,1,0:T(8,128)(2,1)}), bf16[48,8,128]{2,1,0:T(8,128)(2,1)S(1)}, u32[]{:S(2)}, u32[]{:S(2)}) async-start(bf16[48,8,128]{2,1,0:T(8,128)(2,1)} %bitcast), calls=%async_computation | async-start | bytes 196608 | tf_op jit(solution)/shard_map/all_to_all | solution.py:329
  28.5 0.0 copy-done.3
  28.5 0.1 copy.10
  28.6 0.0 copy-done.4
  28.6 0.1 copy.9
  28.7 14.0 %all-to-all-done.u_ref = bf16[48,8,128]{2,1,0:T(8,128)(2,1)S(1)} async-done(((bf16[48,8,128]{2,1,0:T(8,128)(2,1)}), bf16[48,8,128]{2,1,0:T(8,128)(2,1)S(1)}, u32[]{:S(2)}, u32[]{:S(2)}) %all-to-all-start) | async-done | bytes 98336 | tf_op jit(solution)/shard_map/all_to_all | solution.py:329
  42.7 0.0 copy-done.2
  42.7 0.5 mix_heads.1
  43.3 18.3 %all_to_all.15 = bf16[48,8,128]{2,1,0:T(8,128)(2,1)S(1)} all-to-all(bf16[48,8,128]{2,1,0:T(8,128)(2,1)S(1)} %mix_heads.1), channel_id=1, replica_groups=mesh['tensor'=48,'context'=16] {'tensor'}, dimensions={0} | all-to-all | bytes 196608 | tf_op jit(solution)/shard_map/all_to_all | solution.py:329
  61.5 1.0 repeat.1
  62.5 3.9 %all-to-all-start.2 = ((bf16[8,384,128]{2,1,0:T(8,128)(2,1)}), bf16[8,384,128]{2,1,0:T(8,128)(2,1)S(1)}, u32[]{:S(2)}, u32[]{:S(2)}) async-start(bf16[8,384,128]{2,1,0:T(8,128)(2,1)} %repeat.1), calls=%async_computation.2 | async-start | bytes 1572864 | tf_op jit(solution)/shard_map/all_to_all | solution.py:332
  66.4 0.0 copy-start.1
  66.4 1.9 %copy-done.1 = bf16[384,4096]{1,0:T(8,128)(2,1)S(1)} copy-done((bf16[384,4096]{1,0:T(8,128)(2,1)S(1)}, bf16[384,4096]{1,0:T(8,128)(2,1)}, u32[]{:S(2)}) %copy-start.1) | copy-done | bytes 3145752
  68.3 5.7 %project_queries_keys.1 = (bf16[384,128]{1,0:T(8,128)(2,1)}, bf16[1,400,128]{2,1,0:T(8,128)(2,1)S(1)}) custom-call(s32[4]{0:T(128)} %ids_ref.3, bf16[384,8192]{1,0:T(8,128)(2,1)} %x_ref.3, bf16[384,4096]{1,0:T(8,128)(2,1)S(1)} %copy-done.1, bf16[8192,128]{1,0:T(8,128)(2,1)} %wq_ref.1, bf16[8192,128]{1,0:T(8,128)(2,1)} %wk_ref.1), custom_call_target="tpu_custom_call" | custom-call | tf_op jit(solution)/shard_map/project_queries_keys/pallas_call | solution.py:114
  74.0 3.4 %collective-permute-start = (bf16[1,400,128]{2,1,0:T(8,128)(2,1)S(1)}, bf16[1,400,128]{2,1,0:T(8,128)(2,1)S(1)}, u32[]{:S(2)}, u32[]{:S(2)}) collective-permute-start(bf16[1,400,128]{2,1,0:T(8,128)(2,1)S(1)} %get-tuple-element.15.refs_0_), channel_id=1, source_target_pairs={{0,2},{1,3},{2,0},{3,1},{4,6},{5,7},{6,4},{7,5},{8,10},{9,11},{10,... | collective-permute-start | bytes 307208 | tf_op jit(solution)/shard_map/ppermute | solution.py:337
  77.4 2.3 %collective-permute-done.refs_1_ = bf16[1,400,128]{2,1,0:T(8,128)(2,1)S(1)} collective-permute-done((bf16[1,400,128]{2,1,0:T(8,128)(2,1)S(1)}, bf16[1,400,128]{2,1,0:T(8,128)(2,1)S(1)}, u32[]{:S(2)}, u32[]{:S(2)}) %collective-permute-start) | collective-permute-done | bytes 102432 | tf_op jit(solution)/shard_map/ppermute | solution.py:337
  79.7 3.1 %collective-permute-start.1 = (bf16[2,400,128]{2,1,0:T(8,128)(2,1)S(1)}, bf16[2,400,128]{2,1,0:T(8,128)(2,1)S(1)}, u32[]{:S(2)}, u32[]{:S(2)}) collective-permute-start(bf16[2,400,128]{2,1,0:T(8,128)(2,1)S(1)} %pack.2.refs_0_), channel_id=1, source_target_pairs={{0,4},{1,5},{2,6},{3,7},{4,0},{5,1},{6,2},{7,3},{8,12},{9,13},{10,... | collective-permute-start | bytes 614408 | tf_op jit(solution)/shard_map/ppermute | solution.py:337
  82.8 3.7 %collective-permute-start.2 = (bf16[2,400,128]{2,1,0:T(8,128)(2,1)S(1)}, bf16[2,400,128]{2,1,0:T(8,128)(2,1)S(1)}, u32[]{:S(2)}, u32[]{:S(2)}) collective-permute-start(bf16[2,400,128]{2,1,0:T(8,128)(2,1)S(1)} %pack.2.refs_0_), channel_id=1, source_target_pairs={{0,12},{1,13},{2,14},{3,15},{4,8},{5,9},{6,10},{7,11},{8,4},{9,5},... | collective-permute-start | bytes 614408 | tf_op jit(solution)/shard_map/ppermute | solution.py:337
  86.5 2.5 %collective-permute-start.3 = (bf16[2,400,128]{2,1,0:T(8,128)(2,1)S(1)}, bf16[2,400,128]{2,1,0:T(8,128)(2,1)S(1)}, u32[]{:S(2)}, u32[]{:S(2)}) collective-permute-start(bf16[2,400,128]{2,1,0:T(8,128)(2,1)S(1)} %pack.2.refs_0_), channel_id=1, source_target_pairs={{0,8},{1,9},{2,10},{3,11},{4,12},{5,13},{6,14},{7,15},{8,0},{9,1},... | collective-permute-start | bytes 614408 | tf_op jit(solution)/shard_map/ppermute | solution.py:337
  89.1 0.0 collective-permute-done.1.refs_1_
  89.1 1.5 %collective-permute-done.2.refs_2_ = bf16[2,400,128]{2,1,0:T(8,128)(2,1)S(1)} collective-permute-done((bf16[2,400,128]{2,1,0:T(8,128)(2,1)S(1)}, bf16[2,400,128]{2,1,0:T(8,128)(2,1)S(1)}, u32[]{:S(2)}, u32[]{:S(2)}) %collective-permute-start.2) | collective-permute-done | bytes 204832 | tf_op jit(solution)/shard_map/ppermute | solution.py:337
  90.5 5.8 %collective-permute-done.3.refs_3_ = bf16[2,400,128]{2,1,0:T(8,128)(2,1)S(1)} collective-permute-done((bf16[2,400,128]{2,1,0:T(8,128)(2,1)S(1)}, bf16[2,400,128]{2,1,0:T(8,128)(2,1)S(1)}, u32[]{:S(2)}, u32[]{:S(2)}) %collective-permute-start.3) | collective-permute-done | bytes 204832 | tf_op jit(solution)/shard_map/ppermute | solution.py:337
  96.3 0.1 pack.3.refs_0_
  96.4 7.1 %collective-permute-start.4 = (bf16[8,400,128]{2,1,0:T(8,128)(2,1)S(1)}, bf16[8,400,128]{2,1,0:T(8,128)(2,1)S(1)}, u32[]{:S(2)}, u32[]{:S(2)}) collective-permute-start(bf16[8,400,128]{2,1,0:T(8,128)(2,1)S(1)} %pack.3.refs_0_), channel_id=1, source_target_pairs={{0,1},{1,0},{2,3},{3,2},{4,5},{5,4},{6,7},{7,6},{8,9},{9,8},{10,11... | collective-permute-start | bytes 2457608 | tf_op jit(solution)/shard_map/ppermute | solution.py:337
  103.5 0.0 all-to-all-done.2.v_ref
  103.5 1.9 %collective-permute-start.5 = (bf16[8,384,128]{2,1,0:T(8,128)(2,1)S(1)}, bf16[8,384,128]{2,1,0:T(8,128)(2,1)S(1)}, u32[]{:S(2)}, u32[]{:S(2)}) collective-permute-start(bf16[8,384,128]{2,1,0:T(8,128)(2,1)S(1)} %all-to-all-done.2.v_ref), channel_id=1, source_target_pairs={{0,1},{1,0},{2,3},{3,2},{4,5},{5,4},{6,7},{7,6},{8,9},{9,8},{10,11... | collective-permute-start | bytes 2359304 | tf_op jit(solution)/shard_map/ppermute | solution.py:337
  105.4 0.0 collective-permute-done.4.refs_1_
  105.4 3.6 %attention_weights.1 = (bf16[2,192,3072]{2,1,0:T(8,128)(2,1)S(1)}, f32[384,128]{1,0:T(8,128)}) custom-call(s32[4]{0:T(128)} %ids_ref.3, bf16[384,128]{1,0:T(8,128)(2,1)} %get-tuple-element.14.q_ref, bf16[8,400,128]{2,1,0:T(8,128)(2,1)S(1)} %pack.3.refs_0_, bf16[8,400,128]{2,1,0:T(8,128)(2,1)S(1)} %collective-permute-done.4.refs_1_), custom_call_target="tpu_custom_call" | custom-call | tf_op jit(solution)/shard_map/attention_weights/pallas_call | solution.py:213
  109.0 1.4 %apply_first.1 = (f32[384,128]{1,0:T(8,128)S(1)}, f32[384,128]{1,0:T(8,128)S(1)}) custom-call(bf16[2,192,3072]{2,1,0:T(8,128)(2,1)S(1)} %get-tuple-element.16.w_ref, f32[384,128]{1,0:T(8,128)} %get-tuple-element.17.total_ref, bf16[8,384,128]{2,1,0:T(8,128)(2,1)S(1)} %all-to-all-done.2.v_ref), custom_call_target="tpu_custom_call" | custom-call | tf_op jit(solution)/shard_map/apply_first/pallas_call | solution.py:261
  110.4 0.0 collective-permute-done.5.v_ref
  110.4 1.1 %apply_last.1 = bf16[384,128]{1,0:T(8,128)(2,1)} custom-call(bf16[2,192,3072]{2,1,0:T(8,128)(2,1)S(1)} %get-tuple-element.16.w_ref, f32[384,128]{1,0:T(8,128)S(1)} %get-tuple-element.19.total_ref, f32[384,128]{1,0:T(8,128)S(1)} %get-tuple-element.20.part_ref, bf16[8,384,128]{2,1,0:T(8,128)(2,1)S(1)} %collective-permute-done.5.v_ref), custom_call_target="tpu_custom_call" | custom-call | tf_op jit(solution)/shard_map/apply_last/pallas_call | solution.py:272
  (2 shorter events, 0.0 us)
Async XLA Ops:
  0.0 28.5 %copy-start.3 = (bf16[48,96]{1,0:T(8,128)(2,1)S(1)}, bf16[48,96]{1,0:T(8,128)(2,1)}, u32[]{:S(2)}) copy-start(bf16[48,96]{1,0:T(8,128)(2,1)} %param.13) | copy-start | bytes 27652
  0.0 28.6 %copy-start.4 = (bf16[48,96]{1,0:T(8,128)(2,1)S(1)}, bf16[48,96]{1,0:T(8,128)(2,1)}, u32[]{:S(2)}) copy-start(bf16[48,96]{1,0:T(8,128)(2,1)} %param.12) | copy-start | bytes 27652
  0.0 42.7 %copy-start.2 = (bf16[96,48]{0,1:T(8,128)(2,1)S(1)}, bf16[96,48]{0,1:T(8,128)(2,1)}, u32[]{:S(2)}) copy-start(bf16[96,48]{0,1:T(8,128)(2,1)} %param.14) | copy-start | bytes 27652
  5.2 1.6 %copy-start = (bf16[384,4096]{1,0:T(8,128)(2,1)}, bf16[384,4096]{1,0:T(8,128)(2,1)S(1)}, u32[]{:S(2)}) copy-start(bf16[384,4096]{1,0:T(8,128)(2,1)S(1)} %get-tuple-element.13.kept_ref) | copy-start | bytes 9437188
  6.8 35.9 %all-to-all-start = ((bf16[48,8,128]{2,1,0:T(8,128)(2,1)}), bf16[48,8,128]{2,1,0:T(8,128)(2,1)S(1)}, u32[]{:S(2)}, u32[]{:S(2)}) async-start(bf16[48,8,128]{2,1,0:T(8,128)(2,1)} %bitcast), calls=%async_computation | async-start | bytes 196608 | tf_op jit(solution)/shard_map/all_to_all | solution.py:329
  62.5 41.0 %all-to-all-start.2 = ((bf16[8,384,128]{2,1,0:T(8,128)(2,1)}), bf16[8,384,128]{2,1,0:T(8,128)(2,1)S(1)}, u32[]{:S(2)}, u32[]{:S(2)}) async-start(bf16[8,384,128]{2,1,0:T(8,128)(2,1)} %repeat.1), calls=%async_computation.2 | async-start | bytes 1572864 | tf_op jit(solution)/shard_map/all_to_all | solution.py:332
  66.4 1.9 %copy-start.1 = (bf16[384,4096]{1,0:T(8,128)(2,1)S(1)}, bf16[384,4096]{1,0:T(8,128)(2,1)}, u32[]{:S(2)}) copy-start(bf16[384,4096]{1,0:T(8,128)(2,1)} %copy-done) | copy-start | bytes 9437188
  74.0 5.7 %collective-permute-start = (bf16[1,400,128]{2,1,0:T(8,128)(2,1)S(1)}, bf16[1,400,128]{2,1,0:T(8,128)(2,1)S(1)}, u32[]{:S(2)}, u32[]{:S(2)}) collective-permute-start(bf16[1,400,128]{2,1,0:T(8,128)(2,1)S(1)} %get-tuple-element.15.refs_0_), channel_id=1, source_target_pairs={{0,2},{1,3},{2,0},{3,1},{4,6},{5,7},{6,4},{7,5},{8,10},{9,11},{10,... | collective-permute-start | bytes 307208 | tf_op jit(solution)/shard_map/ppermute | solution.py:337
  79.7 9.3 %collective-permute-start.1 = (bf16[2,400,128]{2,1,0:T(8,128)(2,1)S(1)}, bf16[2,400,128]{2,1,0:T(8,128)(2,1)S(1)}, u32[]{:S(2)}, u32[]{:S(2)}) collective-permute-start(bf16[2,400,128]{2,1,0:T(8,128)(2,1)S(1)} %pack.2.refs_0_), channel_id=1, source_target_pairs={{0,4},{1,5},{2,6},{3,7},{4,0},{5,1},{6,2},{7,3},{8,12},{9,13},{10,... | collective-permute-start | bytes 614408 | tf_op jit(solution)/shard_map/ppermute | solution.py:337
  82.8 7.7 %collective-permute-start.2 = (bf16[2,400,128]{2,1,0:T(8,128)(2,1)S(1)}, bf16[2,400,128]{2,1,0:T(8,128)(2,1)S(1)}, u32[]{:S(2)}, u32[]{:S(2)}) collective-permute-start(bf16[2,400,128]{2,1,0:T(8,128)(2,1)S(1)} %pack.2.refs_0_), channel_id=1, source_target_pairs={{0,12},{1,13},{2,14},{3,15},{4,8},{5,9},{6,10},{7,11},{8,4},{9,5},... | collective-permute-start | bytes 614408 | tf_op jit(solution)/shard_map/ppermute | solution.py:337
  86.5 9.8 %collective-permute-start.3 = (bf16[2,400,128]{2,1,0:T(8,128)(2,1)S(1)}, bf16[2,400,128]{2,1,0:T(8,128)(2,1)S(1)}, u32[]{:S(2)}, u32[]{:S(2)}) collective-permute-start(bf16[2,400,128]{2,1,0:T(8,128)(2,1)S(1)} %pack.2.refs_0_), channel_id=1, source_target_pairs={{0,8},{1,9},{2,10},{3,11},{4,12},{5,13},{6,14},{7,15},{8,0},{9,1},... | collective-permute-start | bytes 614408 | tf_op jit(solution)/shard_map/ppermute | solution.py:337
  96.4 9.0 %collective-permute-start.4 = (bf16[8,400,128]{2,1,0:T(8,128)(2,1)S(1)}, bf16[8,400,128]{2,1,0:T(8,128)(2,1)S(1)}, u32[]{:S(2)}, u32[]{:S(2)}) collective-permute-start(bf16[8,400,128]{2,1,0:T(8,128)(2,1)S(1)} %pack.3.refs_0_), channel_id=1, source_target_pairs={{0,1},{1,0},{2,3},{3,2},{4,5},{5,4},{6,7},{7,6},{8,9},{9,8},{10,11... | collective-permute-start | bytes 2457608 | tf_op jit(solution)/shard_map/ppermute | solution.py:337
  103.5 6.9 %collective-permute-start.5 = (bf16[8,384,128]{2,1,0:T(8,128)(2,1)S(1)}, bf16[8,384,128]{2,1,0:T(8,128)(2,1)S(1)}, u32[]{:S(2)}, u32[]{:S(2)}) collective-permute-start(bf16[8,384,128]{2,1,0:T(8,128)(2,1)S(1)} %all-to-all-done.2.v_ref), channel_id=1, source_target_pairs={{0,1},{1,0},{2,3},{3,2},{4,5},{5,4},{6,7},{7,6},{8,9},{9,8},{10,11... | collective-permute-start | bytes 2359304 | tf_op jit(solution)/shard_map/ppermute | solution.py:337
